TPU v7x, 512 devices: a whole 4x4x16 slice. The times are simulated.
512 devices in a mesh: row: 32 (over z, y_lo), col: 8 (over x, core), rep: 2 (over y_hi).
Axes of the slice: x: 4, y: 4 (y_hi: 2, y_lo: 2; y = y_hi * 2 + y_lo), z: 16, core: 2. Of those that a mesh axis runs over, the one named last changes fastest.
Arguments:
- left_values: float32 [32, 2, 8, 2, 8, 2, 128, 128], P('row', 'rep', 'col'), may hold values from -0.5 to 0.5
- left_rows: int32 [32, 2, 8, 2, 8, 2], P('row', 'rep', 'col'), may hold values from 0 to 3, as said below
- right_values: float32 [2, 32, 8, 8, 4, 128, 128], P('rep', 'row', 'col'), may hold values from -1.5 to 1.5
- right_cols: int32 [2, 32, 8, 8, 4], P('rep', 'row', 'col'), may hold values from 0 to 7
- result_slots: int32 [32, 8, 24], P('row', 'col'), may hold values from 0 to 31, as said below
Outputs:
- result_blocks: float32 [32, 8, 24, 128, 128], P('row', 'col', 'rep')
Inputs may be any that keep to these rules, and one draw needn't show every extreme that they name: `result_slots`: within one result tile the 24 slots are distinct; slot value p stands for the block at block row p // 8 and block column p % 8 of the tile. `left_rows`: the 2 block rows of one block column of a panel are distinct.
All inputs are finite; a program needn't handle non-finite values.
Results may differ from a plain program's by a relative error of at most 0.0003.
Values sent between devices are 32-bit elements; how exact they have to be, the bound alone decides.
A program may use at most 64 MiB of HBM per device.

v0:
```python
import jax
import jax.numpy as jnp
from jax import lax
from jax.sharding import PartitionSpec as P

STEPS = 4
CB = 8


highest = lax.Precision.HIGHEST


def from_behind(x, axis, by):
    peers = lax.axis_size(axis)
    return lax.ppermute(x, axis, [(i, (i + by) % peers) for i in range(peers)])


def turn_products(left_blocks, left_places, right_blocks, right_places, listed):
    products = jnp.einsum("kaxy,kbyz->kabxz", left_blocks, right_blocks, precision=highest)
    block_codes = left_places[:, :, None] * CB + right_places[:, None, :]
    onehot = (block_codes[:, :, :, None] == listed[None, None, None, :]).astype(jnp.float32)
    return jnp.einsum("kabc,kabxz->cxz", onehot, products, precision=highest)


def shards(left_values, left_rows, right_values, right_cols, result_slots):
    column_count = lax.axis_size("col")
    column_at = lax.axis_index("col")
    panels = left_values[0, 0, 0]
    panel_rows = left_rows[0, 0, 0]
    right_first = right_values[0, 0, 0]
    right_first_cols = right_cols[0, 0, 0]
    listed = result_slots[0, 0]
    totals = jnp.zeros((listed.shape[0], panels.shape[-2], panels.shape[-1]), jnp.float32)
    held_values = panels
    held_rows = panel_rows
    right_blocks = right_first
    right_places = right_first_cols
    for turn_index in range(STEPS):
        if turn_index > 0:
            held_values, held_rows = from_behind((held_values, held_rows), "col", -1)
        slot_index = (column_at + turn_index) // column_count
        left_blocks = lax.dynamic_index_in_dim(held_values, slot_index, 0, keepdims=False)
        left_places = lax.dynamic_index_in_dim(held_rows, slot_index, 0, keepdims=False)
        if turn_index > 0:
            right_blocks, right_places = from_behind((right_blocks, right_places), "row", -1)
        totals = totals + turn_products(
            left_blocks, left_places, right_blocks, right_places, listed
        )
    shares = lax.psum_scatter(totals, "rep", scatter_dimension=0, tiled=True)
    return shares[None, None]


def solution(mesh):
    in_specs = (
        P("row", "rep", "col", None, None, None, None, None),
        P("row", "rep", "col", None, None, None),
        P("rep", "row", "col", None, None, None, None),
        P("rep", "row", "col", None, None),
        P("row", "col", None),
    )
    out_specs = P("row", "col", "rep", None, None)
    return jax.shard_map(shards, mesh=mesh, in_specs=in_specs, out_specs=out_specs, check_vma=False)
```

profile of v0, /device:TPU:1, one launch (start us, length us, event | category | flops | bytes accessed | tf_op | source)
XLA Modules:
  0.0 233.3 jit_solution(16534960256324888903)
XLA Ops:
  6.5 0.0 reduce-scatter.2.cloned.1.call-start
  6.5 13.0 %collective-permute-start.3 = (f32[8,4,128,128]{3,2,1,0:T(8,128)}, f32[8,4,128,128]{3,2,1,0:T(8,128)S(1)}, u32[]{:S(2)}, u32[]{:S(2)}) collective-permute-start(f32[8,4,128,128]{3,2,1,0:T(8,128)} %bitcast.112), channel_id=1, source_target_pairs={{0,496},{16,0},{32,16},{48,32},{64,48},{80,64},{96,80},{112,96},{1... | collective-permute-start | bytes 6291464 | tf_op jit(solution)/shard_map/ppermute | solution.py:15
  19.5 1.0 collective-permute-start.2
  20.5 43.6 %collective-permute-done.3 = f32[8,4,128,128]{3,2,1,0:T(8,128)S(1)} collective-permute-done((f32[8,4,128,128]{3,2,1,0:T(8,128)}, f32[8,4,128,128]{3,2,1,0:T(8,128)S(1)}, u32[]{:S(2)}, u32[]{:S(2)}) %collective-permute-start.3) | collective-permute-done | bytes 2097184 | tf_op jit(solution)/shard_map/ppermute | solution.py:15
  64.1 6.1 %collective-permute-start.7 = (f32[8,4,128,128]{3,2,1,0:T(8,128)S(1)}, f32[8,4,128,128]{3,2,1,0:T(8,128)}, u32[]{:S(2)}, u32[]{:S(2)}) collective-permute-start(f32[8,4,128,128]{3,2,1,0:T(8,128)S(1)} %collective-permute-done.3), channel_id=1, source_target_pairs={{0,496},{16,0},{32,16},{48,32},{64,48},{80,64},{96,80},{112,96},{1... | collective-permute-start | bytes 6291464 | tf_op jit(solution)/shard_map/ppermute | solution.py:15
  70.2 0.0 collective-permute-done.2
  70.2 1.8 collective-permute-start.6
  72.0 1.9 collective-permute-start.1
  74.0 1.3 collective-permute-start
  75.3 0.7 fusion.43
  76.0 0.7 broadcast_add_fusion.3
  76.7 7.4 %convolution_bitcast_fusion.3 = f32[8,2,4,128,128]{4,3,2,1,0:T(8,128)} fusion(f32[1,1,1,8,4,128,128]{6,5,4,3,2,1,0:T(8,128)} %param.7, f32[1,1,1,2,8,2,128,128]{7,6,5,4,3,2,1,0:T(8,128)} %param.5, s32[]{:T(128)S(6)} %select_n.33), kind=kOutput, calls=%fused_computation.11 | convolution fusion | flops 1610612736 | bytes 7340036 | tf_op jit(solution)/shard_map/kaxy,kbyz->kabxz/dot_general | solution.py:19
  84.1 29.5 %collective-permute-done.1 = s32[8,4]{0,1:T(4,128)S(1)} collective-permute-done((s32[8,4]{0,1:T(4,128)}, s32[8,4]{0,1:T(4,128)S(1)}, u32[]{:S(2)}, u32[]{:S(2)}) %collective-permute-start.1) | collective-permute-done | bytes 160 | tf_op jit(solution)/shard_map/ppermute | solution.py:15
  113.6 6.3 %collective-permute-start.5 = (s32[8,4]{0,1:T(4,128)S(1)}, s32[8,4]{0,1:T(4,128)S(1)}, u32[]{:S(2)}, u32[]{:S(2)}) collective-permute-start(s32[8,4]{0,1:T(4,128)S(1)} %collective-permute-done.1), channel_id=1, source_target_pairs={{0,496},{16,0},{32,16},{48,32},{64,48},{80,64},{96,80},{112,96},{1... | collective-permute-start | bytes 392 | tf_op jit(solution)/shard_map/ppermute | solution.py:15
  119.9 0.0 collective-permute-done
  119.9 2.7 %collective-permute-start.4 = (s32[2,8,2]{1,2,0:T(2,128)S(1)}, s32[2,8,2]{1,2,0:T(2,128)S(1)}, u32[]{:S(2)}, u32[]{:S(2)}) collective-permute-start(s32[2,8,2]{1,2,0:T(2,128)S(1)} %collective-permute-done), channel_id=1, source_target_pairs={{0,14},{2,0},{4,2},{6,4},{8,6},{10,8},{12,10},{14,12},{1,15},{3,1}... | collective-permute-start | bytes 392 | tf_op jit(solution)/shard_map/ppermute | solution.py:15
  122.7 0.0 collective-permute-done.5
  122.7 3.7 %collective-permute-start.9 = (s32[8,4]{0,1:T(4,128)S(1)}, s32[8,4]{0,1:T(4,128)S(1)}, u32[]{:S(2)}, u32[]{:S(2)}) collective-permute-start(s32[8,4]{0,1:T(4,128)S(1)} %collective-permute-done.5), channel_id=1, source_target_pairs={{0,496},{16,0},{32,16},{48,32},{64,48},{80,64},{96,80},{112,96},{1... | collective-permute-start | bytes 392 | tf_op jit(solution)/shard_map/ppermute | solution.py:15
  126.3 0.0 collective-permute-done.4
  126.4 3.9 %collective-permute-start.8 = (s32[2,8,2]{1,2,0:T(2,128)S(1)}, s32[2,8,2]{1,2,0:T(2,128)S(1)}, u32[]{:S(2)}, u32[]{:S(2)}) collective-permute-start(s32[2,8,2]{1,2,0:T(2,128)S(1)} %collective-permute-done.4), channel_id=1, source_target_pairs={{0,14},{2,0},{4,2},{6,4},{8,6},{10,8},{12,10},{14,12},{1,15},{3,1}... | collective-permute-start | bytes 392 | tf_op jit(solution)/shard_map/ppermute | solution.py:15
  130.2 0.0 collective-permute-done.7
  130.2 2.1 collective-permute-start.11
  132.3 0.0 collective-permute-done.6
  132.4 0.0 collective-permute-start.10
  132.4 0.2 collective-permute-done.8
  132.6 0.0 collective-permute-done.9
  132.6 0.0 copy-start.1
  132.6 5.0 %convolution_bitcast_fusion.2 = f32[8,2,4,128,128]{4,3,2,1,0:T(8,128)S(1)} fusion(f32[8,4,128,128]{3,2,1,0:T(8,128)S(1)} %collective-permute-done.3, f32[2,8,2,128,128]{4,3,2,1,0:T(8,128)} %collective-permute-done.2, s32[]{:T(128)S(6)} %select_n.35), kind=kOutput, calls=%fused_computation.10 | convolution fusion | flops 1610612736 | bytes 7340036 | tf_op jit(solution)/shard_map/kaxy,kbyz->kabxz/dot_general | solution.py:19
  137.6 0.0 copy-done.1
  137.6 4.0 %fusion.4 = f32[24,128,128,1,1]{2,0,4,1,3:T(8,128)S(1)} fusion(f32[8,2,4,128,128]{4,3,2,1,0:T(8,128)S(1)} %convolution_bitcast_fusion.2, s32[8,2,4]{0,2,1:T(4,128)S(1)} %broadcast_add_fusion.2, s32[24]{0:T(128)S(1)} %bitcast.114), kind=kOutput, calls=%fused_computation.4 | convolution fusion | flops 301991424 | bytes 5767520 | tf_op jit(solution)/shard_map/kabc,kabxz->cxz/dot_general | solution.py:22
  141.6 5.6 %convolution_bitcast_fusion.1 = f32[8,2,4,128,128]{4,3,2,1,0:T(8,128)S(1)} fusion(f32[8,4,128,128]{3,2,1,0:T(8,128)} %collective-permute-done.7, f32[2,8,2,128,128]{4,3,2,1,0:T(8,128)} %collective-permute-done.6, s32[]{:T(128)S(6)} %select_n.37), kind=kOutput, calls=%fused_computation.9 | convolution fusion | flops 1610612736 | bytes 7340036 | tf_op jit(solution)/shard_map/kaxy,kbyz->kabxz/dot_general | solution.py:19
  147.3 4.2 %fusion.2 = f32[24,128,128,1,1]{2,0,4,1,3:T(8,128)S(1)} fusion(f32[8,2,4,128,128]{4,3,2,1,0:T(8,128)S(1)} %convolution_bitcast_fusion.1, s32[8,2,4]{0,2,1:T(4,128)S(1)} %broadcast_add_fusion.1, s32[24]{0:T(128)S(1)} %bitcast.115), kind=kOutput, calls=%fused_computation.2 | convolution fusion | flops 301991424 | bytes 5767520 | tf_op jit(solution)/shard_map/kabc,kabxz->cxz/dot_general | solution.py:22
  151.5 28.0 %collective-permute-done.11 = f32[8,4,128,128]{3,2,1,0:T(8,128)S(1)} collective-permute-done((f32[8,4,128,128]{3,2,1,0:T(8,128)}, f32[8,4,128,128]{3,2,1,0:T(8,128)S(1)}, u32[]{:S(2)}, u32[]{:S(2)}) %collective-permute-start.11) | collective-permute-done | bytes 2097184 | tf_op jit(solution)/shard_map/ppermute | solution.py:15
  179.6 0.0 collective-permute-done.10
  179.6 3.7 %convolution_bitcast_fusion = f32[8,2,4,128,128]{4,3,2,1,0:T(8,128)S(1)} fusion(f32[8,4,128,128]{3,2,1,0:T(8,128)S(1)} %collective-permute-done.11, f32[2,8,2,128,128]{4,3,2,1,0:T(8,128)S(1)} %collective-permute-done.10, s32[]{:T(128)S(6)} %select_n.39), kind=kOutput, calls=%fused_computation.8 | convolution fusion | flops 1610612736 | bytes 7340036 | tf_op jit(solution)/shard_map/kaxy,kbyz->kabxz/dot_general | solution.py:19
  183.3 0.0 copy-start
  183.3 4.0 %fusion = f32[24,128,128,1,1]{2,0,4,1,3:T(8,128)S(1)} fusion(f32[8,2,4,128,128]{4,3,2,1,0:T(8,128)S(1)} %convolution_bitcast_fusion, s32[8,2,4]{0,2,1:T(4,128)S(1)} %broadcast_add_fusion, s32[24]{0:T(128)S(1)} %bitcast.116), kind=kOutput, calls=%fused_computation | convolution fusion | flops 301991424 | bytes 5767520 | tf_op jit(solution)/shard_map/kabc,kabxz->cxz/dot_general | solution.py:22
  187.4 0.0 copy-done
  187.4 4.6 %bitcast_add_fusion = f32[24,128,128]{2,0,1:T(8,128)S(1)} fusion(f32[24,128,128,1,1]{2,0,4,1,3:T(8,128)S(1)} %fusion, f32[24,128,128,1,1]{2,0,4,1,3:T(8,128)S(1)} %fusion.2, f32[24,128,128,1,1]{2,0,4,1,3:T(8,128)S(1)} %fusion.4, f32[8,2,4,128,128]{4,3,2,1,0:T(8,128)S(1)} %copy-done, s32[24]{0:T(128)S(1)} %bitcast.117, s32[8,2,4]{0,2,1:T(4,128)S(1)} %broadcast_add_fusion.3), kind=kOutput, calls=%fused_computation.16 | convolution fusion | flops 303171072 | bytes 10486112 | tf_op jit(solution)/shard_map/kabc,kabxz->cxz/dot_general | solution.py:22
  192.0 1.5 copy.7
  193.5 0.0 reduce-scatter.2.cloned.1.call-update
  193.5 33.0 %reduce-scatter.2.cloned.1.call-done = f32[12,128,128]{2,1,0:T(8,128)} async-done(((f32[24,128,128]{2,1,0:T(8,128)}), f32[12,128,128]{2,1,0:T(8,128)}) %reduce-scatter.2.cloned.1.call-update) | async-done | bytes 786448 | tf_op jit(solution)/shard_map/reduce_scatter | solution.py:49
  (6 shorter events, 0.0 us)
Async XLA Ops:
  6.5 219.9 %reduce-scatter.2.cloned.1.call-start = ((), (), s32[]{:S(2)}) async-start(), calls=%async_computation.1 | async-start | bytes 2359296 | tf_op jit(solution)/shard_map/reduce_scatter | solution.py:49
  6.5 57.6 %collective-permute-start.3 = (f32[8,4,128,128]{3,2,1,0:T(8,128)}, f32[8,4,128,128]{3,2,1,0:T(8,128)S(1)}, u32[]{:S(2)}, u32[]{:S(2)}) collective-permute-start(f32[8,4,128,128]{3,2,1,0:T(8,128)} %bitcast.112), channel_id=1, source_target_pairs={{0,496},{16,0},{32,16},{48,32},{64,48},{80,64},{96,80},{112,96},{1... | collective-permute-start | bytes 6291464 | tf_op jit(solution)/shard_map/ppermute | solution.py:15
  19.5 50.7 %collective-permute-start.2 = (f32[2,8,2,128,128]{4,3,2,1,0:T(8,128)}, f32[2,8,2,128,128]{4,3,2,1,0:T(8,128)}, u32[]{:S(2)}, u32[]{:S(2)}) collective-permute-start(f32[2,8,2,128,128]{4,3,2,1,0:T(8,128)} %bitcast.113), channel_id=1, source_target_pairs={{0,14},{2,0},{4,2},{6,4},{8,6},{10,8},{12,10},{14,12},{1,15},{3,1}... | collective-permute-start | bytes 6291464 | tf_op jit(solution)/shard_map/ppermute | solution.py:15
  64.1 66.2 %collective-permute-start.7 = (f32[8,4,128,128]{3,2,1,0:T(8,128)S(1)}, f32[8,4,128,128]{3,2,1,0:T(8,128)}, u32[]{:S(2)}, u32[]{:S(2)}) collective-permute-start(f32[8,4,128,128]{3,2,1,0:T(8,128)S(1)} %collective-permute-done.3), channel_id=1, source_target_pairs={{0,496},{16,0},{32,16},{48,32},{64,48},{80,64},{96,80},{112,96},{1... | collective-permute-start | bytes 6291464 | tf_op jit(solution)/shard_map/ppermute | solution.py:15
  70.2 62.1 %collective-permute-start.6 = (f32[2,8,2,128,128]{4,3,2,1,0:T(8,128)}, f32[2,8,2,128,128]{4,3,2,1,0:T(8,128)}, u32[]{:S(2)}, u32[]{:S(2)}) collective-permute-start(f32[2,8,2,128,128]{4,3,2,1,0:T(8,128)} %collective-permute-done.2), channel_id=1, source_target_pairs={{0,14},{2,0},{4,2},{6,4},{8,6},{10,8},{12,10},{14,12},{1,15},{3,1}... | collective-permute-start | bytes 6291464 | tf_op jit(solution)/shard_map/ppermute | solution.py:15
  72.0 41.5 %collective-permute-start.1 = (s32[8,4]{0,1:T(4,128)}, s32[8,4]{0,1:T(4,128)S(1)}, u32[]{:S(2)}, u32[]{:S(2)}) collective-permute-start(s32[8,4]{0,1:T(4,128)} %bitcast.118), channel_id=1, source_target_pairs={{0,496},{16,0},{32,16},{48,32},{64,48},{80,64},{96,80},{112,96},{1... | collective-permute-start | bytes 392 | tf_op jit(solution)/shard_map/ppermute | solution.py:15
  74.0 46.0 %collective-permute-start = (s32[2,8,2]{1,2,0:T(2,128)}, s32[2,8,2]{1,2,0:T(2,128)S(1)}, u32[]{:S(2)}, u32[]{:S(2)}) collective-permute-start(s32[2,8,2]{1,2,0:T(2,128)} %bitcast.120), channel_id=1, source_target_pairs={{0,14},{2,0},{4,2},{6,4},{8,6},{10,8},{12,10},{14,12},{1,15},{3,1}... | collective-permute-start | bytes 392 | tf_op jit(solution)/shard_map/ppermute | solution.py:15
  113.6 9.1 %collective-permute-start.5 = (s32[8,4]{0,1:T(4,128)S(1)}, s32[8,4]{0,1:T(4,128)S(1)}, u32[]{:S(2)}, u32[]{:S(2)}) collective-permute-start(s32[8,4]{0,1:T(4,128)S(1)} %collective-permute-done.1), channel_id=1, source_target_pairs={{0,496},{16,0},{32,16},{48,32},{64,48},{80,64},{96,80},{112,96},{1... | collective-permute-start | bytes 392 | tf_op jit(solution)/shard_map/ppermute | solution.py:15
  119.9 6.4 %collective-permute-start.4 = (s32[2,8,2]{1,2,0:T(2,128)S(1)}, s32[2,8,2]{1,2,0:T(2,128)S(1)}, u32[]{:S(2)}, u32[]{:S(2)}) collective-permute-start(s32[2,8,2]{1,2,0:T(2,128)S(1)} %collective-permute-done), channel_id=1, source_target_pairs={{0,14},{2,0},{4,2},{6,4},{8,6},{10,8},{12,10},{14,12},{1,15},{3,1}... | collective-permute-start | bytes 392 | tf_op jit(solution)/shard_map/ppermute | solution.py:15
  122.7 9.9 %collective-permute-start.9 = (s32[8,4]{0,1:T(4,128)S(1)}, s32[8,4]{0,1:T(4,128)S(1)}, u32[]{:S(2)}, u32[]{:S(2)}) collective-permute-start(s32[8,4]{0,1:T(4,128)S(1)} %collective-permute-done.5), channel_id=1, source_target_pairs={{0,496},{16,0},{32,16},{48,32},{64,48},{80,64},{96,80},{112,96},{1... | collective-permute-start | bytes 392 | tf_op jit(solution)/shard_map/ppermute | solution.py:15
  126.4 6.3 %collective-permute-start.8 = (s32[2,8,2]{1,2,0:T(2,128)S(1)}, s32[2,8,2]{1,2,0:T(2,128)S(1)}, u32[]{:S(2)}, u32[]{:S(2)}) collective-permute-start(s32[2,8,2]{1,2,0:T(2,128)S(1)} %collective-permute-done.4), channel_id=1, source_target_pairs={{0,14},{2,0},{4,2},{6,4},{8,6},{10,8},{12,10},{14,12},{1,15},{3,1}... | collective-permute-start | bytes 392 | tf_op jit(solution)/shard_map/ppermute | solution.py:15
  130.2 49.3 %collective-permute-start.11 = (f32[8,4,128,128]{3,2,1,0:T(8,128)}, f32[8,4,128,128]{3,2,1,0:T(8,128)S(1)}, u32[]{:S(2)}, u32[]{:S(2)}) collective-permute-start(f32[8,4,128,128]{3,2,1,0:T(8,128)} %collective-permute-done.7), channel_id=1, source_target_pairs={{0,496},{16,0},{32,16},{48,32},{64,48},{80,64},{96,80},{112,96},{1... | collective-permute-start | bytes 6291464 | tf_op jit(solution)/shard_map/ppermute | solution.py:15
  132.4 47.2 %collective-permute-start.10 = (f32[2,8,2,128,128]{4,3,2,1,0:T(8,128)}, f32[2,8,2,128,128]{4,3,2,1,0:T(8,128)S(1)}, u32[]{:S(2)}, u32[]{:S(2)}) collective-permute-start(f32[2,8,2,128,128]{4,3,2,1,0:T(8,128)} %collective-permute-done.6), channel_id=1, source_target_pairs={{0,14},{2,0},{4,2},{6,4},{8,6},{10,8},{12,10},{14,12},{1,15},{3,1}... | collective-permute-start | bytes 6291464 | tf_op jit(solution)/shard_map/ppermute | solution.py:15
  132.6 5.0 %copy-start.1 = (s32[1,1,24]{2,1,0:T(1,128)S(1)}, s32[1,1,24]{2,1,0:T(1,128)}, u32[]{:S(2)}) copy-start(s32[1,1,24]{2,1,0:T(1,128)} %param.9) | copy-start | bytes 292
  183.3 4.1 %copy-start = (f32[8,2,4,128,128]{4,3,2,1,0:T(8,128)S(1)}, f32[8,2,4,128,128]{4,3,2,1,0:T(8,128)}, u32[]{:S(2)}) copy-start(f32[8,2,4,128,128]{4,3,2,1,0:T(8,128)} %convolution_bitcast_fusion.3) | copy-start | bytes 12582916
Sparse Core Ops, SparseCore 0:
  193.6 32.7 reduce-scatter.1
where the time goes:
time: 234 us; the launch traced here: 233 us
  waiting for transfers between devices  134 us (57%)
  starting transfers between devices  43.8 us (19%)
  matrix products  38.6 us (16%)
  between operations  13.6 us (6%)
    ppermute x12, waiting for transfers between devices, from_behind(): return lax.ppermute(x, axis, [(i, (i + by) % peers) for i in range(peers)])  101 us
    ppermute x12, starting transfers between devices, from_behind(): return lax.ppermute(x, axis, [(i, (i + by) % peers) for i in range(peers)])  43.8 us
    reduce_scatter x1, waiting for transfers between devices, shards(): shares = lax.psum_scatter(totals, 'rep', scatter_dimension=0, tiled=True)  33 us
    dot_general x4, matrix products, turn_products(): jnp.einsum('kaxy,kbyz->kabxz', left_blocks, right_blocks, precision=highest)  21.8 us
    dot_general x4, matrix products, turn_products(): return jnp.einsum('kabc,kabxz->cxz', onehot, products, precision=highest)  16.9 us
  transfers between devices with their start and end apart: 13, of which 5 were waited for; matrix products, arithmetic and copies ran while one was open for 12% of the time, Pallas kernels for 0%

commit v1 on v0

v1 whole, which is shorter than its diff:
```python
import functools

import jax
import jax.numpy as jnp
from jax import lax
from jax.experimental import pallas as pl
from jax.experimental.pallas import tpu as pltpu
from jax.sharding import PartitionSpec as P

BS = 128
KB = 8
BPR = 4
LPB = 2
RB = 4
CB = 8
NC = 24
STRIPS = 4
LANES = BS // STRIPS
HALF = KB // 2
OWNED = NC // 2
PACKS = OWNED // STRIPS
UNIT = HALF * BS + 8
PANEL = HALF * LPB * BS + 8
STAGES = 3 * STRIPS
MESH = pl.DeviceIdType.MESH
f32 = jnp.float32
bf16 = jnp.bfloat16


def lane_group():
    return lax.broadcasted_iota(jnp.int32, (BS, BS), 1) // LANES


def regroup(group, parts):
    picked = parts[STRIPS - 1]
    for b in range(STRIPS - 2, -1, -1):
        picked = jnp.where(group == b, parts[b], picked)
    return picked


def shifted(x, groups):
    by = (groups * LANES) % BS
    return x if by == 0 else pltpu.roll(x, by, 1)


def kernel(
    rows, columns,
    left_hbm, right_hbm, left_rows, right_cols, slots, out,
    raw, units, panels, left_hi, left_lo, right_hi, right_lo, sums,
    own, stage, relay, arrived,
    load_sem, left_load_sem, z_send, z_recv, y_send, y_recv, x_send, x_recv,
    hop_send, hop_recv, last_send, last_recv,
):
    row = lax.axis_index("row")
    col = lax.axis_index("col")
    rep = lax.axis_index("rep")
    odd = lax.rem(row, 2)
    core = lax.rem(col, 2)
    chip = lax.div(col, 2)
    chips = columns // 2
    even_row = odd == 0
    even_core = core == 0
    mate_row = row + 1 - 2 * odd
    up = (lax.rem(row + 2, rows), col, rep)
    down = (lax.rem(row + rows - 2, rows), col, rep)
    inner = (mate_row, col, rep)
    outer = (mate_row, col, 1 - rep)
    sibling = (row, col + 1 - 2 * core, rep)
    right = (row, lax.rem(col + 2, columns), rep)
    left = (row, lax.rem(col + columns - 2, columns), rep)
    far = (row, lax.rem(col - core + 4, columns) + 1 - core, rep)

    barrier = pltpu.get_barrier_semaphore()
    peers = (up, down, inner, outer, sibling, right, left, far)
    for peer in peers:
        pl.semaphore_signal(barrier, inc=1, device_id=peer, device_id_type=MESH)

    def load_right(half):
        part = pl.ds(half * HALF * BPR, HALF * BPR)
        return pltpu.make_async_copy(right_hbm.at[part], raw.at[part], load_sem.at[half])

    def load_left(slot, half):
        return pltpu.make_async_copy(
            left_hbm.at[slot, half],
            panels.at[4 * slot, half, pl.ds(0, HALF * LPB * BS)],
            left_load_sem.at[slot, half],
        )

    for half in range(2):
        load_right(half).start()
    for slot in range(2):
        for half in range(2):
            load_left(slot, half).start()

    group = lane_group()
    sub8 = lax.broadcasted_iota(jnp.int32, (8, BS), 0)
    group8 = lax.broadcasted_iota(jnp.int32, (8, BS), 1) // LANES

    for half in range(2):
        marks = jnp.zeros((8, BS), f32)
        for kk in range(HALF):
            for b in range(BPR):
                place = right_cols[(half * HALF + kk) * BPR + b].astype(f32)
                marks = jnp.where((sub8 == kk) & (group8 == b), place, marks)
        for h in range(STRIPS):
            units[h, half, pl.ds(HALF * BS, 8), :] = marks
    for slot in range(2):
        for half in range(2):
            marks = jnp.zeros((8, BS), f32)
            for e in range(HALF * LPB):
                place = left_rows[(slot * KB + half * HALF) * LPB + e].astype(f32)
                marks = jnp.where(sub8 == e, place, marks)
            panels[4 * slot, half, pl.ds(HALF * LPB * BS, 8), :] = marks

    def pack(h, half):
        def one(kk, carry):
            k = half * HALF + kk
            parts = [shifted(raw[k * BPR + b], b - h) for b in range(BPR)]
            units[h, half, pl.ds(pl.multiple_of(kk * BS, BS), BS), :] = regroup(group, parts)
            return carry

        lax.fori_loop(0, HALF, one, 0)

    def z_copy(g, source, target):
        h = lax.div(g, 3)
        return pltpu.make_async_remote_copy(
            src_ref=units.at[h, source], dst_ref=units.at[h, target],
            send_sem=z_send.at[g], recv_sem=z_recv.at[g], device_id=down, device_id_type=MESH,
        )

    def y_copy(g, source, target):
        h = lax.div(g, 3)
        return pltpu.make_async_remote_copy(
            src_ref=units.at[h, source], dst_ref=units.at[h, target],
            send_sem=y_send.at[g], recv_sem=y_recv.at[g], device_id=inner, device_id_type=MESH,
        )

    def x_copy(turn_index, half, source, peer, lane):
        return pltpu.make_async_remote_copy(
            src_ref=panels.at[source, half], dst_ref=panels.at[turn_index, half],
            send_sem=x_send.at[lane, half], recv_sem=x_recv.at[turn_index - 1, half],
            device_id=peer, device_id_type=MESH,
        )

    def hop_copy(h, way):
        return pltpu.make_async_remote_copy(
            src_ref=stage.at[h, way], dst_ref=relay.at[h, way],
            send_sem=hop_send.at[h, way], recv_sem=hop_recv.at[h, way],
            device_id=(inner, outer)[way], device_id_type=MESH,
        )

    def last_copy(h, way):
        return pltpu.make_async_remote_copy(
            src_ref=relay.at[h, way], dst_ref=arrived.at[h, way],
            send_sem=last_send.at[h, way], recv_sem=last_recv.at[h, way],
            device_id=(outer, inner)[way], device_id_type=MESH,
        )

    load_right(0).wait()
    pack(0, 0)
    load_right(1).wait()
    pack(0, 1)
    pl.semaphore_wait(barrier, len(peers))

    @pl.when(even_row)
    def _():
        z_copy(0, 0, 4).start()
        z_copy(1, 1, 5).start()

    @pl.when(odd == 1)
    def _():
        y_copy(0, 0, 2).start()
        z_copy(0, 1, 5).start()
        y_copy(1, 1, 3).start()

    for slot in range(2):
        for half in range(2):
            load_left(slot, half).wait()

    near_slot = jnp.where(chip == 0, 4, 0)
    far_slot = jnp.where(chip < 2, 4, 0)
    for half in range(2):
        x_copy(2, half, near_slot, left, 0).start()

    @pl.when(even_core)
    def _():
        for half in range(2):
            x_copy(3, half, far_slot, far, 1).start()

    @pl.when(core == 1)
    def _():
        for half in range(2):
            x_copy(1, half, 0, sibling, 1).start()

    for h in range(1, STRIPS):
        for half in range(2):
            pack(h, half)

    sums[...] = jnp.zeros_like(sums)

    def fill_left(turn_index, half):
        def one(kk, carry):
            marks = panels[turn_index, half, pl.ds(HALF * LPB * BS, 8), :]
            at = pl.ds(pl.multiple_of(kk * BS, BS), BS)
            first = panels[turn_index, half, pl.ds(pl.multiple_of(kk * LPB * BS, BS), BS), :]
            second = panels[turn_index, half, pl.ds(pl.multiple_of(kk * LPB * BS + BS, BS), BS), :]
            mark_row = lambda e: jnp.sum(jnp.where(sub8 == e, marks, 0.0), axis=0, keepdims=True)
            first_row = jnp.broadcast_to(mark_row(kk * LPB), (BS, BS))
            second_row = jnp.broadcast_to(mark_row(kk * LPB + 1), (BS, BS))
            for r in range(RB):
                block = jnp.where(first_row == r, first, jnp.where(second_row == r, second, 0.0))
                hi = block.astype(bf16)
                left_hi[turn_index, half, r, :, at] = hi
                left_lo[turn_index, half, r, :, at] = (block - hi.astype(f32)).astype(bf16)
            return carry

        lax.fori_loop(0, HALF, one, 0)

    fill_left(0, 0)
    fill_left(0, 1)

    def products(h, unit):
        turn_index = lax.div(unit, 2)
        half = lax.rem(unit, 2)

        def fill(kk, carry):
            marks = units[h, unit, pl.ds(HALF * BS, 8), :]
            mine = jnp.sum(jnp.where(sub8 == kk, marks, 0.0), axis=0, keepdims=True)
            mine = jnp.broadcast_to(mine, (8, BS))
            at = pl.ds(pl.multiple_of(kk * BS, BS), BS)
            packed = units[h, unit, at, :]
            for u in range(2):
                total = None
                for turned in range(STRIPS):
                    place = jnp.broadcast_to(shifted(mine, STRIPS - turned)[:1], (BS, BS))
                    term = jnp.where(place == (group + 4 * u).astype(f32), shifted(packed, STRIPS - turned), 0.0)
                    total = term if total is None else total + term
                hi = total.astype(bf16)
                right_hi[at, u * BS:(u + 1) * BS] = hi
                right_lo[at, u * BS:(u + 1) * BS] = (total - hi.astype(f32)).astype(bf16)
            return carry

        lax.fori_loop(0, HALF, fill, 0)
        l_hi = left_hi[turn_index, half].reshape(RB * BS, HALF * BS)
        l_lo = left_lo[turn_index, half].reshape(RB * BS, HALF * BS)
        got = jnp.dot(l_hi, right_hi[...], preferred_element_type=f32)
        got += jnp.dot(l_lo, right_hi[...], preferred_element_type=f32)
        got += jnp.dot(l_hi, right_lo[...], preferred_element_type=f32)
        for u in range(2):
            for r in range(RB):
                sums[h * CB + u * RB + r] += got[r * BS:(r + 1) * BS, u * BS:(u + 1) * BS]

    def gather(h, first, keep):
        def one(q, carry):
            parts = []
            for b in range(STRIPS):
                slot = slots[first + q * STRIPS + b]
                r = lax.div(slot, CB)
                c = lax.rem(slot, CB)
                block = sums[h * CB + lax.div(c, 4) * RB + r]
                away = lax.rem(b - lax.rem(c, 4) + STRIPS, STRIPS)
                placed = block
                for groups in range(1, STRIPS):
                    placed = jnp.where(away == groups, shifted(block, groups), placed)
                parts.append(placed)
            whole = regroup(group, parts)
            keep[h, 0, q] = whole[:BS // 2]
            keep[h, 1, q] = whole[BS // 2:]
            return carry

        lax.fori_loop(0, PACKS, one, 0)

    def pass_on(h):
        for way in range(2):
            hop_copy(h, way).wait_recv()
            last_copy(h, way).start()

    def step(g, carry):
        h = lax.div(g, 3)
        s = lax.rem(g, 3)
        z_unit = 4 + s + odd
        y_unit = jnp.where(s < 2, 2 + s, 7 - 3 * odd)
        more = g < STAGES - 3

        z_copy(g, z_unit, z_unit).wait_recv()

        @pl.when(even_row)
        def _():
            y_copy(g, z_unit, 2 + s).start()

        @pl.when((odd == 1) & (s == 0))
        def _():
            y_copy(g + 2, z_unit, 7).start()

        y_copy(g, y_unit, y_unit).wait_recv()

        @pl.when(even_row & (s == 0))
        def _():
            z_copy(g + 2, y_unit, 6).start()

        @pl.when((odd == 1) & (s < 2))
        def _():
            z_copy(g + 1, y_unit, 6 + s).start()

        @pl.when(even_row & (s > 0) & more)
        def _():
            z_copy(g + 2, s - 1, 3 + s).start()

        @pl.when((odd == 1) & (s > 0) & more)
        def _():
            y_copy(g + 2, s - 1, 1 + s).start()

        @pl.when((odd == 1) & (s == 1) & more)
        def _():
            z_copy(g + 2, 1, 5).start()

        @pl.when(g == 4)
        def _():
            for half in range(2):
                x_copy(2, half, 0, left, 0).wait_recv()

            @pl.when(even_core)
            def _():
                for half in range(2):
                    x_copy(1, half, 2, sibling, 2).start()

            @pl.when(core == 1)
            def _():
                for half in range(2):
                    x_copy(3, half, 2, sibling, 2).start()

        @pl.when(g == 5)
        def _():
            for half in range(2):
                x_copy(1, half, 0, sibling, 1).wait_recv()
                x_copy(3, half, 0, sibling, 1).wait_recv()

            def one(i, c):
                fill_left(1 + lax.div(i, 2), lax.rem(i, 2))
                return c

            lax.fori_loop(0, 6, one, 0)

        for at, strip in ((7, 0), (9, 1), (10, 2)):
            @pl.when(g == at)
            def _():
                pass_on(strip)

        def done(at):
            late = jnp.where(at == 8, 24, jnp.where(at == 9, 28, 10 + 2 * at))
            return jnp.where(at < 2, at + 1, jnp.where(at < 5, 2, jnp.where(at < 8, 6 * at - 22, late)))

        start = done(g - 1)

        def task(i, c):
            q = start + i

            @pl.when(q < done(g))
            def _():
                th = lax.div(q, 8)
                j = lax.rem(q, 8)
                ts = lax.div(j + 6, 2) - 4
                from_z = 4 + ts + odd
                from_y = jnp.where(ts < 2, 2 + ts, 7 - 3 * odd)
                unit = jnp.where(j < 2, j, jnp.where(lax.rem(j, 2) == 0, from_z, from_y))
                products(th, unit)

            return c

        lax.fori_loop(0, 6, task, 0)

        @pl.when((g == 5) | (g == 7) | (g == 8) | (g == 11))
        def _():
            strip = jnp.where(g == 5, 0, jnp.where(g == 7, 1, jnp.where(g == 8, 2, 3)))
            gather(strip, OWNED * (1 - rep), stage)
            for way in range(2):
                hop_copy(strip, way).start()
            gather(strip, OWNED * rep, own)

        return carry

    lax.fori_loop(0, STAGES, step, 0)
    pass_on(STRIPS - 1)

    def finish_wait(h, carry):
        for way in range(2):
            last_copy(h, way).wait_recv()
        return carry

    lax.fori_loop(0, STRIPS, finish_wait, 0)
    group_half = group[:BS // 2]

    def finish(i, carry):
        q = lax.div(i, 2)
        way = lax.rem(i, 2)
        whole = [own[h, way, q] + arrived[h, way, q] for h in range(STRIPS)]
        at = pl.ds(pl.multiple_of(way * (BS // 2), BS // 2), BS // 2)
        for b in range(STRIPS):
            out[q * STRIPS + b, at, :] = regroup(group_half, [shifted(whole[h], h - b) for h in range(STRIPS)])
        return carry

    lax.fori_loop(0, 2 * PACKS, finish, 0)

    def z_sent(g, carry):
        z_copy(g, 0, 0).wait_send()
        y_copy(g, 0, 0).wait_send()
        return carry

    lax.fori_loop(0, STAGES, z_sent, 0)
    for lane in range(3):
        for half in range(2):
            x_lane_sent(x_copy, lane, half, left)
    for h in range(STRIPS):
        for way in range(2):
            hop_copy(h, way).wait_send()
            last_copy(h, way).wait_send()


def x_lane_sent(x_copy, lane, half, peer):
    x_copy(1, half, 0, peer, lane).wait_send()


def shards(rows, columns, left_values, left_rows, right_values, right_cols, result_slots):
    left = left_values.reshape(2, 2, HALF * LPB * BS, BS)
    right = right_values.reshape(KB * BPR, BS, BS)
    vmem = pltpu.VMEM
    dma = pltpu.SemaphoreType.DMA
    out = pl.pallas_call(
        functools.partial(kernel, rows, columns),
        out_shape=jax.ShapeDtypeStruct((OWNED, BS, BS), f32),
        in_specs=[
            pl.BlockSpec(memory_space=pl.ANY),
            pl.BlockSpec(memory_space=pl.ANY),
            pl.BlockSpec(memory_space=pltpu.SMEM),
            pl.BlockSpec(memory_space=pltpu.SMEM),
            pl.BlockSpec(memory_space=pltpu.SMEM),
        ],
        out_specs=pl.BlockSpec(memory_space=vmem),
        scratch_shapes=[
            vmem((KB * BPR, BS, BS), f32),
            vmem((STRIPS, 8, UNIT, BS), f32),
            vmem((5, 2, PANEL, BS), f32),
            vmem((4, 2, RB, BS, HALF * BS), bf16),
            vmem((4, 2, RB, BS, HALF * BS), bf16),
            vmem((HALF * BS, 2 * BS), bf16),
            vmem((HALF * BS, 2 * BS), bf16),
            vmem((STRIPS * CB, BS, BS), f32),
            vmem((STRIPS, 2, PACKS, BS // 2, BS), f32),
            vmem((STRIPS, 2, PACKS, BS // 2, BS), f32),
            vmem((STRIPS, 2, PACKS, BS // 2, BS), f32),
            vmem((STRIPS, 2, PACKS, BS // 2, BS), f32),
            dma((2,)), dma((2, 2)),
            dma((STAGES,)), dma((STAGES,)), dma((STAGES,)), dma((STAGES,)),
            dma((3, 2)), dma((3, 2)),
            dma((STRIPS, 2)), dma((STRIPS, 2)), dma((STRIPS, 2)), dma((STRIPS, 2)),
        ],
        compiler_params=pltpu.CompilerParams(
            collective_id=0, has_side_effects=True, vmem_limit_bytes=48 * 2**20
        ),
    )(left, right, left_rows.reshape(-1), right_cols.reshape(-1), result_slots.reshape(-1))
    return out[None, None]


def solution(mesh):
    in_specs = (
        P("row", "rep", "col", None, None, None, None, None),
        P("row", "rep", "col", None, None, None),
        P("rep", "row", "col", None, None, None, None),
        P("rep", "row", "col", None, None),
        P("row", "col", None),
    )
    out_specs = P("row", "col", "rep", None, None)
    body = functools.partial(shards, mesh.shape["row"], mesh.shape["col"])
    return jax.shard_map(body, mesh=mesh, in_specs=in_specs, out_specs=out_specs, check_vma=False)
```

time: 234 us -> 133 us (0.57)
  the two profiles are of different devices: /device:TPU:1 before, /device:TPU:74 now
where the time goes in v1:
time: 133 us; the launch traced here: 132 us
  Pallas kernels  126 us (95%)
  local copies, waits for them, and re-layouts  6.4 us (5%)
    pallas_call x1, Pallas kernels, shards(): pl.pallas_call(functools.partial(kernel, rows, columns), out_shape=jax.Sh...  126 us
    unnamed x9, local copies, waits for them, and re-layouts  6.23 us

profile of v1, /device:TPU:74, one launch (start us, length us, event | category | flops | bytes accessed | tf_op | source)
XLA Modules:
  0.0 132.4 jit_solution(6164222735145961403)
XLA Ops:
  0.0 0.8 copy.9
  0.8 0.1 reshape.18.right_cols
  0.8 0.8 copy.8
  1.6 0.1 reshape.17.left_rows
  1.7 0.0 copy-start
  1.7 1.6 %copy-done = f32[1,1,1,2,8,2,128,128]{7,6,5,4,3,2,1,0:T(8,128)S(1)} copy-done((f32[1,1,1,2,8,2,128,128]{7,6,5,4,3,2,1,0:T(8,128)S(1)}, f32[1,1,1,2,8,2,128,128]{7,6,5,4,3,2,1,0:T(8,128)}, u32[]{:S(2)}) %copy-start) | copy-done | bytes 2097176
  3.3 0.0 copy-start.1
  3.3 1.6 %copy-done.1 = f32[1,1,1,8,4,128,128]{6,5,4,3,2,1,0:T(8,128)S(1)} copy-done((f32[1,1,1,8,4,128,128]{6,5,4,3,2,1,0:T(8,128)S(1)}, f32[1,1,1,8,4,128,128]{6,5,4,3,2,1,0:T(8,128)}, u32[]{:S(2)}) %copy-start.1) | copy-done | bytes 2097176
  4.9 0.0 copy-start.2
  4.9 0.7 copy-done.2
  5.5 126.0 %shard_map.55 = f32[12,128,128]{2,1,0:T(8,128)S(1)} custom-call(f32[2,2,1024,128]{3,2,1,0:T(8,128)S(1)} %bitcast.9, f32[32,128,128]{2,1,0:T(8,128)S(1)} %bitcast.10, s32[32]{0:T(128)S(1)} %reshape.17.left_rows, s32[32]{0:T(128)S(1)} %reshape.18.right_cols, s32[24]{0:T(128)S(1)} %bitcast.11), custom_call_target="tpu_custom_call" | custom-call | tf_op jit(solution)/shard_map/pallas_call | solution.py:428
  131.5 0.9 copy.11
Async XLA Ops:
  1.7 1.6 %copy-start = (f32[1,1,1,2,8,2,128,128]{7,6,5,4,3,2,1,0:T(8,128)S(1)}, f32[1,1,1,2,8,2,128,128]{7,6,5,4,3,2,1,0:T(8,128)}, u32[]{:S(2)}) copy-start(f32[1,1,1,2,8,2,128,128]{7,6,5,4,3,2,1,0:T(8,128)} %param.5) | copy-start | bytes 6291460
  3.3 1.6 %copy-start.1 = (f32[1,1,1,8,4,128,128]{6,5,4,3,2,1,0:T(8,128)S(1)}, f32[1,1,1,8,4,128,128]{6,5,4,3,2,1,0:T(8,128)}, u32[]{:S(2)}) copy-start(f32[1,1,1,8,4,128,128]{6,5,4,3,2,1,0:T(8,128)} %param.7) | copy-start | bytes 6291460
  4.9 0.7 copy-start.2

commit v2 on v0

v2 whole, which is shorter than its diff:
```python
import functools

import jax
import jax.numpy as jnp
from jax import lax
from jax.experimental import pallas as pl
from jax.experimental.pallas import tpu as pltpu
from jax.sharding import PartitionSpec as P

BS = 128
KB = 8
BPR = 4
LPB = 2
RB = 4
CB = 8
NC = 24
STRIPS = 4
LANES = BS // STRIPS
OWNED = NC // 2
PACKS = OWNED // STRIPS
QUARTERS = 4
DEPTH = KB // QUARTERS * BS
TASKS = 4 * QUARTERS
SLAB = 32
VMEM_LIMIT = 60 * 2**20
MESH = pl.DeviceIdType.MESH
f32 = jnp.float32
bf16 = jnp.bfloat16

SLOT = {
    "zE0": (0, 0, 1), "zE1": (1, 1, 1), "zE2": (2, 2, 1), "zE3": (3, 3, 1), "zA": (4, 0, 1), "zB": (4, 1, 2), "zD": (5, 3, 1),
    "yE0": (0, 0, 1), "yE1": (1, 1, 1), "yE2": (2, 2, 1), "yE3": (3, 3, 1), "yA": (4, 0, 1),
    "oA": (0, 0, 1), "oB": (1, 1, 2), "oD": (2, 3, 1), "ob": (3, 1, 2),
}
WAITS = {
    0: [('zE0', 2), ('zE1', 2), ('zE2', 2), ('oA', 1), ('oD', 1), ('zE3', 2), ('zA', 3), ('oB', 1), ('zD', 3), ('ob', 3)],
    1: [('yE0', 1), ('yE1', 1), ('zB', 2), ('yE2', 1), ('yE3', 1), ('zE0', 3), ('zD', 2), ('zE2', 3), ('yA', 2), ('zE1', 3), ('zE3', 3)],
}
RELAYS = {
    0: {"zE0": ("yE0", 2, 1), "zE1": ("yE1", 2, 1), "zE2": ("yE2", 2, 1), "zE3": ("yE3", 2, 1),
        "zA": ("yA", 3, 2), "oA": ("zA", 1, 3), "oD": ("zD", 1, 3)},
    1: {"zB": ("ob", 2, 3), "yE0": ("zE0", 1, 3), "yE1": ("zE1", 1, 3), "yE2": ("zE2", 1, 3), "yE3": ("zE3", 1, 3)},
}
OWN = {
    0: [('zE0', 2, 0), ('zE1', 2, 4), ('zE2', 2, 6), ('zE3', 2, 9)],
    1: [('oD', 1, 1), ('zD', 2, 3), ('zB', 2, 4), ('oA', 1, 4), ('oB', 1, 5)],
}
STEPS = 11
PASS_ON = {0: [31, 40, 39], 1: [36, 31, 36]}
LEFT_RELAY = {0: 14, 1: 14}
LEFT_READY = {0: 17, 1: 17}
DONE = {
    0: [1, 2, 3, 4, 4, 4, 4, 4, 4, 4, 4, 4, 4, 4, 4, 4, 4, 6, 8, 10, 12, 12, 15, 18, 21, 24, 27, 30, 33, 36, 39, 42, 42, 45, 48, 51, 54, 57, 58, 59, 61, 62, 64, 64],
    1: [1, 2, 3, 4, 4, 4, 4, 4, 4, 4, 4, 4, 4, 4, 4, 4, 4, 7, 10, 13, 16, 19, 22, 25, 28, 31, 34, 37, 40, 43, 46, 47, 48, 50, 52, 54, 56, 58, 59, 60, 61, 62, 63, 64],
}
ORDER = {
    0: [0, 1, 2, 3, 8, 9, 10, 4, 7, 11, 12, 5, 6, 15, 13, 14],
    1: [0, 1, 2, 3, 4, 5, 9, 10, 6, 7, 12, 11, 14, 8, 13, 15],
}
MOST = max(b - a for role in (0, 1) for a, b in zip([0] + DONE[role], DONE[role]))


def by_role(odd, even_value, odd_value):
    return even_value + odd * (odd_value - even_value)


def lookup(index, values):
    found = jnp.int32(values[0])
    for at in range(1, len(values)):
        if values[at] != values[at - 1]:
            found = found + jnp.where(index >= at, values[at] - values[at - 1], 0)
    return found


def regroup(group, parts):
    picked = parts[STRIPS - 1]
    for b in range(STRIPS - 2, -1, -1):
        picked = jnp.where(group == b, parts[b], picked)
    return picked


def shifted(x, groups):
    by = (groups * LANES) % BS
    return x if by == 0 else pltpu.roll(x, by, 1)


def sum_of_dots(left_parts, right_parts, turn_index, quarter):
    left = jnp.concatenate([left_parts[turn_index, quarter, part] for part in range(3)], axis=1)
    right = right_parts[...].reshape(3 * DEPTH, 2 * BS)
    return jnp.dot(left, right, preferred_element_type=f32)


def kernel(
    rows, columns,
    left_hbm, right_hbm, left_rows_hbm, right_cols_hbm, slots_hbm, out,
    raw, units, panels, left_parts, right_parts, sums,
    own, stage, relay, arrived, marks, wheres, left_rows, right_cols, slots,
    load_sem, left_load_sem, small_sem, z_send, z_recv, y_send, y_recv, x_send, x_recv,
    mark_send, mark_recv, hop_send, hop_recv, last_send, last_recv,
):
    row = lax.axis_index("row")
    col = lax.axis_index("col")
    rep = lax.axis_index("rep")
    odd = lax.rem(row, 2)
    core = lax.rem(col, 2)
    chip = lax.div(col, 2)
    is_role = {0: odd == 0, 1: odd == 1}
    mate_row = row + 1 - 2 * odd
    up = (lax.rem(row + 2, rows), col, rep)
    down = (lax.rem(row + rows - 2, rows), col, rep)
    inner = (mate_row, col, rep)
    outer = (mate_row, col, 1 - rep)
    sibling = (row, col + 1 - 2 * core, rep)
    right = (row, lax.rem(col + 2, columns), rep)
    left = (row, lax.rem(col + columns - 2, columns), rep)
    far = (row, lax.rem(col - core + 4, columns) + 1 - core, rep)

    barrier = pltpu.get_barrier_semaphore()
    peers = (up, down, inner, outer, sibling, right, left, far)
    for peer in peers:
        pl.semaphore_signal(barrier, inc=1, device_id=peer, device_id_type=MESH)

    small = [
        pltpu.make_async_copy(right_cols_hbm, right_cols, small_sem.at[0]),
        pltpu.make_async_copy(left_rows_hbm, left_rows, small_sem.at[1]),
        pltpu.make_async_copy(slots_hbm, slots, small_sem.at[2]),
    ]

    def load_right(half):
        part = pl.ds(half * KB * BPR // 2, KB * BPR // 2)
        return pltpu.make_async_copy(right_hbm.at[part], raw.at[part], load_sem.at[half])

    def load_left(slot):
        return pltpu.make_async_copy(
            left_hbm.at[slot], panels.at[4 * slot, pl.ds(0, KB * LPB * BS)], left_load_sem.at[slot]
        )

    small[0].start()
    for half in range(2):
        load_right(half).start()
    small[1].start()
    small[2].start()
    for slot in range(2):
        load_left(slot).start()

    group = lax.broadcasted_iota(jnp.int32, (SLAB, BS), 1) // LANES
    sub8 = lax.broadcasted_iota(jnp.int32, (8, BS), 0)
    group8 = lax.broadcasted_iota(jnp.int32, (8, BS), 1) // LANES

    def pack(h, k):
        for slab in range(0, BS, SLAB):
            parts = [shifted(raw[k * BPR + b, pl.ds(slab, SLAB), :], b - h) for b in range(BPR)]
            at = pl.ds(pl.multiple_of(lax.rem(k, 2) * BS + slab, SLAB), SLAB)
            units[h, lax.div(k, 2), at, :] = regroup(group, parts)

    def unit_copy(link, name, h, source, target):
        slot, first, count = SLOT[name]
        sends, recvs, peer = (z_send, z_recv, down) if link == "z" else (y_send, y_recv, inner)
        return pltpu.make_async_remote_copy(
            src_ref=units.at[h, pl.ds(source * QUARTERS + first, count)],
            dst_ref=units.at[h, pl.ds(target * QUARTERS + first, count)],
            send_sem=sends.at[h, slot], recv_sem=recvs.at[h, slot], device_id=peer, device_id_type=MESH,
        )

    def link_of(name):
        return "z" if name[0] == "z" else "y"

    def x_copy(turn_index, source, peer, lane):
        return pltpu.make_async_remote_copy(
            src_ref=panels.at[source], dst_ref=panels.at[turn_index],
            send_sem=x_send.at[lane], recv_sem=x_recv.at[turn_index - 1],
            device_id=peer, device_id_type=MESH,
        )

    def mark_copy(source, target, peer, lane):
        return pltpu.make_async_remote_copy(
            src_ref=marks.at[source], dst_ref=marks.at[target],
            send_sem=mark_send.at[lane], recv_sem=mark_recv.at[target - 1],
            device_id=peer, device_id_type=MESH,
        )

    def hop_copy(h, way):
        return pltpu.make_async_remote_copy(
            src_ref=stage.at[h, way], dst_ref=relay.at[h, way],
            send_sem=hop_send.at[h, way], recv_sem=hop_recv.at[h, way],
            device_id=(inner, outer)[way], device_id_type=MESH,
        )

    def last_copy(h, way):
        return pltpu.make_async_remote_copy(
            src_ref=relay.at[h, way], dst_ref=arrived.at[h, way],
            send_sem=last_send.at[h, way], recv_sem=last_recv.at[h, way],
            device_id=(outer, inner)[way], device_id_type=MESH,
        )

    small[0].wait()
    places = jnp.zeros((8, BS), f32)
    for b in range(BPR):
        for k in range(KB):
            places = jnp.where((group8 == b) & (sub8 == k), right_cols[b, k].astype(f32), places)
    marks[0] = places

    def pack_first(k, carry):
        pack(0, k)
        return carry

    for half in range(2):
        load_right(half).wait()
        lax.fori_loop(half * KB // 2, (half + 1) * KB // 2, pack_first, 0)
    pl.semaphore_wait(barrier, len(peers))

    for role in (0, 1):
        @pl.when(is_role[role])
        def _():
            if role == 0:
                mark_copy(0, 2, down, 0).start()
            else:
                mark_copy(0, 1, inner, 0).start()
                mark_copy(0, 2, down, 1).start()
            for name, target, _ in OWN[role]:
                unit_copy(link_of(name), name, 0, 0, target).start()

    small[1].wait()
    for slot in range(2):
        load_left(slot).wait()
        for a in range(LPB):
            places = jnp.zeros((8, BS), f32)
            for k in range(KB):
                places = jnp.where(sub8 == k, left_rows[slot, a, k].astype(f32), places)
            panels[4 * slot, pl.ds(KB * LPB * BS + 8 * a, 8), :] = places

    x_copy(2, jnp.where(chip == 0, 4, 0), left, 0).start()

    @pl.when(core == 0)
    def _():
        x_copy(3, jnp.where(chip < 2, 4, 0), far, 1).start()

    @pl.when(core == 1)
    def _():
        x_copy(1, 0, sibling, 1).start()

    def pack_rest(k, carry):
        for h in range(1, STRIPS):
            pack(h, k)
        return carry

    lax.fori_loop(0, KB, pack_rest, 0)
    sums[...] = jnp.zeros_like(sums)
    small[2].wait()

    def row_of(tile, k):
        one = jnp.sum(jnp.where(sub8 == k, tile, 0.0), axis=0, keepdims=True)
        return jnp.broadcast_to(one, (8, BS))

    def tall(x):
        return x.reshape(SLAB // 8, 8, BS)

    def fill_left(turn_index):
        def one(k, carry):
            quarter = lax.div(k, 2)
            at = pl.ds(pl.multiple_of(lax.rem(k, 2) * BS, BS), BS)
            where = [row_of(panels[turn_index, pl.ds(KB * LPB * BS + 8 * a, 8), :], k) for a in range(LPB)]
            for slab in range(0, BS, SLAB):
                blocks = [
                    tall(panels[turn_index, pl.ds(pl.multiple_of((k * LPB + a) * BS + slab, SLAB), SLAB), :])
                    for a in range(LPB)
                ]
                for r in range(RB):
                    second = jnp.where((where[1] == r)[None], blocks[1], 0.0)
                    block = jnp.where((where[0] == r)[None], blocks[0], second).reshape(SLAB, BS)
                    hi = block.astype(bf16)
                    lo = (block - hi.astype(f32)).astype(bf16)
                    for part, value in enumerate((hi, lo, hi)):
                        left_parts[turn_index, quarter, part, pl.ds(r * BS + slab, SLAB), at] = value
            return carry

        lax.fori_loop(0, KB, one, 0)

    def fill_wheres(turn_index):
        tile = marks[turn_index]
        for k in range(KB):
            mine = row_of(tile, k)
            for turned in range(STRIPS):
                wheres[turn_index, k, turned] = shifted(mine, STRIPS - turned)

    fill_left(0)
    fill_wheres(0)

    def products(h, turn_index, quarter):
        for kk in range(KB // QUARTERS):
            places = [wheres[turn_index, quarter * 2 + kk, turned] for turned in range(STRIPS)]
            masks = [[(place == (group8 + 4 * u).astype(f32))[None] for place in places] for u in range(2)]
            for slab in range(0, BS, SLAB):
                at = pl.ds(kk * BS + slab, SLAB)
                packed = units[h, turn_index * QUARTERS + quarter, at, :]
                blocks = [tall(shifted(packed, STRIPS - turned)) for turned in range(STRIPS)]
                for u in range(2):
                    terms = [jnp.where(mask, block, 0.0) for mask, block in zip(masks[u], blocks)]
                    whole = ((terms[0] + terms[1]) + (terms[2] + terms[3])).reshape(SLAB, BS)
                    hi = whole.astype(bf16)
                    lo = (whole - hi.astype(f32)).astype(bf16)
                    for part, value in enumerate((hi, hi, lo)):
                        right_parts[part, at, u * BS:(u + 1) * BS] = value
        got = sum_of_dots(left_parts, right_parts, turn_index, quarter)
        for u in range(2):
            for r in range(RB):
                sums[h * CB + u * RB + r] += got[r * BS:(r + 1) * BS, u * BS:(u + 1) * BS]

    def gather(h, first, keep):
        def one(q, carry):
            found = []
            for b in range(STRIPS):
                slot = slots[0, first + q * STRIPS + b]
                c = lax.rem(slot, CB)
                away = lax.rem(b - lax.rem(c, 4) + STRIPS, STRIPS)
                found.append((h * CB + lax.div(c, 4) * RB + lax.div(slot, CB), away * LANES))
            for slab in range(0, BS, SLAB):
                parts = [pltpu.roll(sums[block, pl.ds(slab, SLAB), :], by, 1) for block, by in found]
                way, at = divmod(slab, BS // 2)
                keep[h, way, q, pl.ds(at, SLAB), :] = regroup(group, parts)
            return carry

        lax.fori_loop(0, PACKS, one, 0)

    def pass_on(h):
        for way in range(2):
            hop_copy(h, way).wait_recv()
            last_copy(h, way).start()

    def step(g, carry):
        h = lax.div(g, STEPS)
        s = lax.rem(g, STEPS)
        for role in (0, 1):
            for at, (name, turn_index) in enumerate(WAITS[role]):
                @pl.when(is_role[role] & (s == at))
                def _():
                    unit_copy(link_of(name), name, h, turn_index, turn_index).wait_recv()
                    sent_on = RELAYS[role].get(name)
                    if sent_on is not None:
                        unit_copy(link_of(sent_on[0]), sent_on[0], h, sent_on[1], sent_on[2]).start()
                    if role == 0 and name == "zE0":
                        @pl.when(h == 0)
                        def _():
                            mark_copy(0, 2, inner, 0).wait_recv()
                            mark_copy(2, 1, inner, 1).start()
                    if role == 1 and name == "yE0":
                        @pl.when(h == 0)
                        def _():
                            mark_copy(0, 1, inner, 0).wait_recv()
                            mark_copy(1, 3, down, 2).start()
                    if role == 1 and name == "zB":
                        @pl.when(h == 0)
                        def _():
                            mark_copy(0, 2, inner, 0).wait_recv()
                            mark_copy(2, 3, inner, 3).start()

                    @pl.when(h < STRIPS - 1)
                    def _():
                        for own_name, target, after in OWN[role]:
                            if after == at:
                                unit_copy(link_of(own_name), own_name, h + 1, 0, target).start()

        @pl.when(g == by_role(odd, LEFT_RELAY[0], LEFT_RELAY[1]))
        def _():
            x_copy(2, 0, left, 0).wait_recv()

            @pl.when(core == 0)
            def _():
                x_copy(1, 2, sibling, 2).start()

            @pl.when(core == 1)
            def _():
                x_copy(3, 2, sibling, 2).start()

        @pl.when(g == by_role(odd, LEFT_READY[0], LEFT_READY[1]))
        def _():
            x_copy(1, 0, sibling, 1).wait_recv()
            x_copy(3, 0, sibling, 1).wait_recv()
            for role in (0, 1):
                @pl.when(is_role[role])
                def _():
                    for turn_index in ((1, 3), (3,))[role]:
                        mark_copy(0, turn_index, inner, 0).wait_recv()

            def one(i, c):
                fill_left(i)
                fill_wheres(i)
                return c

            lax.fori_loop(1, 4, one, 0)

        for strip in range(STRIPS - 1):
            @pl.when(g == by_role(odd, PASS_ON[0][strip], PASS_ON[1][strip]))
            def _():
                pass_on(strip)

        before = by_role(odd, lookup(g, [0] + DONE[0]), lookup(g, [0] + DONE[1]))
        after = by_role(odd, lookup(g, DONE[0]), lookup(g, DONE[1]))

        def task(i, c):
            q = before + i

            @pl.when(q < after)
            def _():
                j = lax.rem(q, TASKS)
                code = by_role(odd, lookup(j, ORDER[0]), lookup(j, ORDER[1]))
                products(lax.div(q, TASKS), lax.div(code, QUARTERS), lax.rem(code, QUARTERS))

            return c

        lax.fori_loop(0, MOST, task, 0)

        @pl.when(lax.div(after, TASKS) > lax.div(before, TASKS))
        def _():
            strip = lax.div(before, TASKS)
            gather(strip, OWNED * (1 - rep), stage)
            for way in range(2):
                hop_copy(strip, way).start()
            gather(strip, OWNED * rep, own)

        return carry

    lax.fori_loop(0, STRIPS * STEPS, step, 0)
    pass_on(STRIPS - 1)

    def finish_wait(h, carry):
        for way in range(2):
            last_copy(h, way).wait_recv()
        return carry

    lax.fori_loop(0, STRIPS, finish_wait, 0)

    def finish(i, carry):
        q = lax.div(i, 2)
        way = lax.rem(i, 2)
        for slab in range(0, BS // 2, SLAB):
            part = pl.ds(slab, SLAB)
            whole = [own[h, way, q, part, :] + arrived[h, way, q, part, :] for h in range(STRIPS)]
            at = pl.ds(pl.multiple_of(way * (BS // 2) + slab, SLAB), SLAB)
            for b in range(STRIPS):
                out[q * STRIPS + b, at, :] = regroup(group, [shifted(whole[h], h - b) for h in range(STRIPS)])
        return carry

    lax.fori_loop(0, 2 * PACKS, finish, 0)

    def sent(h, carry):
        for role in (0, 1):
            @pl.when(is_role[role])
            def _():
                names = [name for name, _, _ in RELAYS[role].values()] + [name for name, _, _ in OWN[role]]
                for name in names:
                    unit_copy(link_of(name), name, h, 0, 0).wait_send()

        for way in range(2):
            hop_copy(h, way).wait_send()
            last_copy(h, way).wait_send()
        return carry

    lax.fori_loop(0, STRIPS, sent, 0)
    for role in (0, 1):
        @pl.when(is_role[role])
        def _():
            for lane in range((2, 4)[role]):
                mark_copy(0, 1, inner, lane).wait_send()
    for lane in range(3):
        x_copy(1, 0, left, lane).wait_send()


def shards(rows, columns, left_values, left_rows, right_values, right_cols, result_slots):
    left = left_values.reshape(2, KB * LPB * BS, BS)
    right = right_values.reshape(KB * BPR, BS, BS)
    vmem = pltpu.VMEM
    dma = pltpu.SemaphoreType.DMA
    out = pl.pallas_call(
        functools.partial(kernel, rows, columns),
        out_shape=jax.ShapeDtypeStruct((OWNED, BS, BS), f32),
        in_specs=[pl.BlockSpec(memory_space=pltpu.HBM)] * 5,
        out_specs=pl.BlockSpec(memory_space=vmem),
        scratch_shapes=[
            vmem((KB * BPR, BS, BS), f32),
            vmem((STRIPS, 4 * QUARTERS, DEPTH, BS), f32),
            vmem((5, KB * LPB * BS + 16, BS), f32),
            vmem((4, QUARTERS, 3, RB * BS, DEPTH), bf16),
            vmem((3, DEPTH, 2 * BS), bf16),
            vmem((STRIPS * CB, BS, BS), f32),
            vmem((STRIPS, 2, PACKS, BS // 2, BS), f32),
            vmem((STRIPS, 2, PACKS, BS // 2, BS), f32),
            vmem((STRIPS, 2, PACKS, BS // 2, BS), f32),
            vmem((STRIPS, 2, PACKS, BS // 2, BS), f32),
            vmem((4, 8, BS), f32),
            vmem((4, KB, STRIPS, 8, BS), f32),
            pltpu.SMEM((2, LPB, KB), jnp.int32),
            pltpu.SMEM((BPR, KB), jnp.int32),
            pltpu.SMEM((1, NC), jnp.int32),
            dma((2,)), dma((2,)), dma((3,)),
            dma((STRIPS, 6)), dma((STRIPS, 6)), dma((STRIPS, 5)), dma((STRIPS, 5)),
            dma((3,)), dma((3,)), dma((4,)), dma((3,)),
            dma((STRIPS, 2)), dma((STRIPS, 2)), dma((STRIPS, 2)), dma((STRIPS, 2)),
        ],
        compiler_params=pltpu.CompilerParams(
            collective_id=0, has_side_effects=True, vmem_limit_bytes=VMEM_LIMIT
        ),
    )(
        left, right, left_rows.reshape(2, KB, LPB).transpose(0, 2, 1), right_cols.reshape(KB, BPR).T,
        result_slots.reshape(1, NC),
    )
    return out[None, None]


def solution(mesh):
    in_specs = (
        P("row", "rep", "col", None, None, None, None, None),
        P("row", "rep", "col", None, None, None),
        P("rep", "row", "col", None, None, None, None),
        P("rep", "row", "col", None, None),
        P("row", "col", None),
    )
    out_specs = P("row", "col", "rep", None, None)
    body = functools.partial(shards, mesh.shape["row"], mesh.shape["col"])
    return jax.shard_map(body, mesh=mesh, in_specs=in_specs, out_specs=out_specs, check_vma=False)
```

time: 234 us -> 117 us (0.50)
  the two profiles are of different devices: /device:TPU:1 before, /device:TPU:14 now
where the time goes in v2:
time: 117 us
  Pallas kernels  115 us (98%)
  local copies, waits for them, and re-layouts  2.06 us (2%)
    pallas_call x1, Pallas kernels, shards(): pl.pallas_call(functools.partial(kernel, rows, columns), out_shape=jax.Sh...  115 us

profile of v2, /device:TPU:14, one launch (start us, length us, event | category | flops | bytes accessed | tf_op | source)
XLA Modules:
  0.0 117.1 jit_solution(15582836261593519132)
XLA Ops:
  0.0 115.1 %shard_map.55 = f32[12,128,128]{2,1,0:T(8,128)} custom-call(f32[2,2048,128]{2,1,0:T(8,128)} %bitcast.11, f32[32,128,128]{2,1,0:T(8,128)} %bitcast.12, s32[2,2,8]{2,1,0:T(2,128)} %bitcast.13, s32[4,8]{1,0:T(4,128)} %bitcast.14, s32[1,24]{1,0:T(1,128)} %bitcast.15), custom_call_target="tpu_custom_call" | custom-call | tf_op jit(solution)/shard_map/pallas_call | solution.py:474
  115.1 2.1 %copy.7 = f32[1,1,12,128,128]{4,3,2,1,0:T(8,128)} copy(f32[1,1,12,128,128]{4,3,2,1,0:T(8,128)} %bitcast.10) | data formatting | bytes 1572864

commit v3 on v2

--- a/solution.py
+++ b/solution.py
@@ -18,23 +18,26 @@
 LANES = BS // STRIPS
 OWNED = NC // 2
 PACKS = OWNED // STRIPS
-QUARTERS = 4
-DEPTH = KB // QUARTERS * BS
-TASKS = 4 * QUARTERS
+HALVES = 2
+HALF = KB // HALVES
+TASKS = 4 * HALVES
 SLAB = 32
 VMEM_LIMIT = 60 * 2**20
 MESH = pl.DeviceIdType.MESH
 f32 = jnp.float32
 bf16 = jnp.bfloat16
 
+IN_A = 2
+IN_B = 4
 SLOT = {
-    "zE0": (0, 0, 1), "zE1": (1, 1, 1), "zE2": (2, 2, 1), "zE3": (3, 3, 1), "zA": (4, 0, 1), "zB": (4, 1, 2), "zD": (5, 3, 1),
-    "yE0": (0, 0, 1), "yE1": (1, 1, 1), "yE2": (2, 2, 1), "yE3": (3, 3, 1), "yA": (4, 0, 1),
-    "oA": (0, 0, 1), "oB": (1, 1, 2), "oD": (2, 3, 1), "ob": (3, 1, 2),
+    "zE0": (0, 0, 2), "zE1": (1, 2, 2), "zE2": (2, 4, 2), "zE3": (3, 6, 2), "zA": (4, 0, IN_A), "zB": (4, IN_A, IN_B),
+    "zD": (5, IN_A + IN_B, KB - IN_A - IN_B),
+    "yE0": (0, 0, 2), "yE1": (1, 2, 2), "yE2": (2, 4, 2), "yE3": (3, 6, 2), "yA": (4, 0, IN_A),
+    "oA": (0, 0, IN_A), "oB": (1, IN_A, IN_B), "oD": (2, IN_A + IN_B, KB - IN_A - IN_B), "ob": (3, IN_A, IN_B),
 }
 WAITS = {
-    0: [('zE0', 2), ('zE1', 2), ('zE2', 2), ('oA', 1), ('oD', 1), ('zE3', 2), ('zA', 3), ('oB', 1), ('zD', 3), ('ob', 3)],
-    1: [('yE0', 1), ('yE1', 1), ('zB', 2), ('yE2', 1), ('yE3', 1), ('zE0', 3), ('zD', 2), ('zE2', 3), ('yA', 2), ('zE1', 3), ('zE3', 3)],
+    0: [('zE0', 2), ('zE1', 2), ('oA', 1), ('oD', 1), ('zE2', 2), ('zE3', 2), ('zA', 3), ('oB', 1), ('zD', 3), ('ob', 3)],
+    1: [('yE0', 1), ('zB', 2), ('yE1', 1), ('yE2', 1), ('zD', 2), ('yE3', 1), ('zE0', 3), ('yA', 2), ('zE2', 3), ('zE1', 3), ('zE3', 3)],
 }
 RELAYS = {
     0: {"zE0": ("yE0", 2, 1), "zE1": ("yE1", 2, 1), "zE2": ("yE2", 2, 1), "zE3": ("yE3", 2, 1),
@@ -42,20 +45,20 @@
     1: {"zB": ("ob", 2, 3), "yE0": ("zE0", 1, 3), "yE1": ("zE1", 1, 3), "yE2": ("zE2", 1, 3), "yE3": ("zE3", 1, 3)},
 }
 OWN = {
-    0: [('zE0', 2, 0), ('zE1', 2, 4), ('zE2', 2, 6), ('zE3', 2, 9)],
-    1: [('oD', 1, 1), ('zD', 2, 3), ('zB', 2, 4), ('oA', 1, 4), ('oB', 1, 5)],
+    0: [('zE0', 2, 4), ('zE1', 2, 5), ('zE2', 2, 8), ('zE3', 2, 8)],
+    1: [('zB', 2, 5), ('oA', 1, 6), ('oD', 1, 6), ('oB', 1, 7), ('zD', 2, 10)],
 }
 STEPS = 11
-PASS_ON = {0: [31, 40, 39], 1: [36, 31, 36]}
+PASS_ON = {0: [42, 42, 40], 1: [35, 36, 35]}
 LEFT_RELAY = {0: 14, 1: 14}
 LEFT_READY = {0: 17, 1: 17}
 DONE = {
-    0: [1, 2, 3, 4, 4, 4, 4, 4, 4, 4, 4, 4, 4, 4, 4, 4, 4, 6, 8, 10, 12, 12, 15, 18, 21, 24, 27, 30, 33, 36, 39, 42, 42, 45, 48, 51, 54, 57, 58, 59, 61, 62, 64, 64],
-    1: [1, 2, 3, 4, 4, 4, 4, 4, 4, 4, 4, 4, 4, 4, 4, 4, 4, 7, 10, 13, 16, 19, 22, 25, 28, 31, 34, 37, 40, 43, 46, 47, 48, 50, 52, 54, 56, 58, 59, 60, 61, 62, 63, 64],
+    0: [1, 2, 2, 2, 2, 2, 2, 2, 2, 2, 2, 2, 2, 2, 2, 2, 2, 4, 6, 8, 10, 10, 11, 12, 13, 14, 15, 16, 17, 18, 19, 20, 20, 23, 26, 27, 27, 27, 28, 28, 30, 30, 32, 32],
+    1: [2, 2, 2, 2, 2, 2, 2, 2, 2, 2, 2, 2, 2, 2, 2, 2, 2, 4, 6, 8, 10, 12, 13, 14, 15, 16, 17, 18, 19, 20, 21, 22, 23, 25, 26, 27, 27, 28, 29, 29, 30, 30, 31, 32],
 }
 ORDER = {
-    0: [0, 1, 2, 3, 8, 9, 10, 4, 7, 11, 12, 5, 6, 15, 13, 14],
-    1: [0, 1, 2, 3, 4, 5, 9, 10, 6, 7, 12, 11, 14, 8, 13, 15],
+    0: [0, 1, 4, 5, 2, 3, 6, 7],
+    1: [0, 1, 2, 5, 3, 4, 6, 7],
 }
 MOST = max(b - a for role in (0, 1) for a, b in zip([0] + DONE[role], DONE[role]))
 
@@ -84,16 +87,10 @@
     return x if by == 0 else pltpu.roll(x, by, 1)
 
 
-def sum_of_dots(left_parts, right_parts, turn_index, quarter):
-    left = jnp.concatenate([left_parts[turn_index, quarter, part] for part in range(3)], axis=1)
-    right = right_parts[...].reshape(3 * DEPTH, 2 * BS)
-    return jnp.dot(left, right, preferred_element_type=f32)
-
-
 def kernel(
     rows, columns,
     left_hbm, right_hbm, left_rows_hbm, right_cols_hbm, slots_hbm, out,
-    raw, units, panels, left_parts, right_parts, sums,
+    raw, units, panels, left_parts, right_first, right_second, sums,
     own, stage, relay, arrived, marks, wheres, left_rows, right_cols, slots,
     load_sem, left_load_sem, small_sem, z_send, z_recv, y_send, y_recv, x_send, x_recv,
     mark_send, mark_recv, hop_send, hop_recv, last_send, last_recv,
@@ -150,15 +147,14 @@
     def pack(h, k):
         for slab in range(0, BS, SLAB):
             parts = [shifted(raw[k * BPR + b, pl.ds(slab, SLAB), :], b - h) for b in range(BPR)]
-            at = pl.ds(pl.multiple_of(lax.rem(k, 2) * BS + slab, SLAB), SLAB)
-            units[h, lax.div(k, 2), at, :] = regroup(group, parts)
+            units[h, 0, pl.ds(pl.multiple_of(k * BS + slab, SLAB), SLAB), :] = regroup(group, parts)
 
     def unit_copy(link, name, h, source, target):
         slot, first, count = SLOT[name]
         sends, recvs, peer = (z_send, z_recv, down) if link == "z" else (y_send, y_recv, inner)
         return pltpu.make_async_remote_copy(
-            src_ref=units.at[h, pl.ds(source * QUARTERS + first, count)],
-            dst_ref=units.at[h, pl.ds(target * QUARTERS + first, count)],
+            src_ref=units.at[h, source, pl.ds(first * BS, count * BS)],
+            dst_ref=units.at[h, target, pl.ds(first * BS, count * BS)],
             send_sem=sends.at[h, slot], recv_sem=recvs.at[h, slot], device_id=peer, device_id_type=MESH,
         )
 
@@ -257,8 +253,8 @@
 
     def fill_left(turn_index):
         def one(k, carry):
-            quarter = lax.div(k, 2)
-            at = pl.ds(pl.multiple_of(lax.rem(k, 2) * BS, BS), BS)
+            half = lax.div(k, HALF)
+            at = pl.ds(pl.multiple_of(lax.rem(k, HALF) * BS, BS), BS)
             where = [row_of(panels[turn_index, pl.ds(KB * LPB * BS + 8 * a, 8), :], k) for a in range(LPB)]
             for slab in range(0, BS, SLAB):
                 blocks = [
@@ -270,8 +266,8 @@
                     block = jnp.where((where[0] == r)[None], blocks[0], second).reshape(SLAB, BS)
                     hi = block.astype(bf16)
                     lo = (block - hi.astype(f32)).astype(bf16)
-                    for part, value in enumerate((hi, lo, hi)):
-                        left_parts[turn_index, quarter, part, pl.ds(r * BS + slab, SLAB), at] = value
+                    for part, value in enumerate((hi, lo)):
+                        left_parts[turn_index, half, part, pl.ds(r * BS + slab, SLAB), at] = value
             return carry
 
         lax.fori_loop(0, KB, one, 0)
@@ -286,22 +282,29 @@
     fill_left(0)
     fill_wheres(0)
 
-    def products(h, turn_index, quarter):
-        for kk in range(KB // QUARTERS):
-            places = [wheres[turn_index, quarter * 2 + kk, turned] for turned in range(STRIPS)]
-            masks = [[(place == (group8 + 4 * u).astype(f32))[None] for place in places] for u in range(2)]
-            for slab in range(0, BS, SLAB):
-                at = pl.ds(kk * BS + slab, SLAB)
-                packed = units[h, turn_index * QUARTERS + quarter, at, :]
-                blocks = [tall(shifted(packed, STRIPS - turned)) for turned in range(STRIPS)]
-                for u in range(2):
-                    terms = [jnp.where(mask, block, 0.0) for mask, block in zip(masks[u], blocks)]
-                    whole = ((terms[0] + terms[1]) + (terms[2] + terms[3])).reshape(SLAB, BS)
-                    hi = whole.astype(bf16)
-                    lo = (whole - hi.astype(f32)).astype(bf16)
-                    for part, value in enumerate((hi, hi, lo)):
-                        right_parts[part, at, u * BS:(u + 1) * BS] = value
-        got = sum_of_dots(left_parts, right_parts, turn_index, quarter)
+    def products(h, turn_index, half):
+        got = None
+        depth = HALF * BS // 2
+        for pair, right_parts in enumerate((right_first, right_second)):
+            for kk in range(2):
+                k = half * HALF + pair * 2 + kk
+                places = [wheres[turn_index, k, turned] for turned in range(STRIPS)]
+                masks = [[(place == (group8 + 4 * u).astype(f32))[None] for place in places] for u in range(2)]
+                for slab in range(0, BS, SLAB):
+                    packed = units[h, turn_index, pl.ds(pl.multiple_of(k * BS + slab, SLAB), SLAB), :]
+                    blocks = [tall(shifted(packed, STRIPS - turned)) for turned in range(STRIPS)]
+                    at = pl.ds(kk * BS + slab, SLAB)
+                    for u in range(2):
+                        terms = [jnp.where(mask, block, 0.0) for mask, block in zip(masks[u], blocks)]
+                        whole = ((terms[0] + terms[1]) + (terms[2] + terms[3])).reshape(SLAB, BS)
+                        hi = whole.astype(bf16)
+                        right_parts[0, at, u * BS:(u + 1) * BS] = hi
+                        right_parts[1, at, u * BS:(u + 1) * BS] = (whole - hi.astype(f32)).astype(bf16)
+        for pair, right_parts in enumerate((right_first, right_second)):
+            for left_part, right_part in ((0, 0), (1, 0), (0, 1)):
+                mine = left_parts[turn_index, half, left_part, :, pair * depth:(pair + 1) * depth]
+                term = jnp.dot(mine, right_parts[right_part], preferred_element_type=f32)
+                got = term if got is None else got + term
         for u in range(2):
             for r in range(RB):
                 sums[h * CB + u * RB + r] += got[r * BS:(r + 1) * BS, u * BS:(u + 1) * BS]
@@ -404,7 +407,7 @@
             def _():
                 j = lax.rem(q, TASKS)
                 code = by_role(odd, lookup(j, ORDER[0]), lookup(j, ORDER[1]))
-                products(lax.div(q, TASKS), lax.div(code, QUARTERS), lax.rem(code, QUARTERS))
+                products(lax.div(q, TASKS), lax.div(code, HALVES), lax.rem(code, HALVES))
 
             return c
 
@@ -478,10 +481,11 @@
         out_specs=pl.BlockSpec(memory_space=vmem),
         scratch_shapes=[
             vmem((KB * BPR, BS, BS), f32),
-            vmem((STRIPS, 4 * QUARTERS, DEPTH, BS), f32),
+            vmem((STRIPS, 4, KB * BS, BS), f32),
             vmem((5, KB * LPB * BS + 16, BS), f32),
-            vmem((4, QUARTERS, 3, RB * BS, DEPTH), bf16),
-            vmem((3, DEPTH, 2 * BS), bf16),
+            vmem((4, 2, 2, RB * BS, HALF * BS), bf16),
+            vmem((2, HALF * BS // 2, 2 * BS), bf16),
+            vmem((2, HALF * BS // 2, 2 * BS), bf16),
             vmem((STRIPS * CB, BS, BS), f32),
             vmem((STRIPS, 2, PACKS, BS // 2, BS), f32),
             vmem((STRIPS, 2, PACKS, BS // 2, BS), f32),

time: 117 us -> 108 us (0.923)
  the two profiles are of different devices: /device:TPU:14 before, /device:TPU:11 now
where the time goes in v3:
time: 108 us
  Pallas kernels  106 us (98%)
  local copies, waits for them, and re-layouts  2.06 us (2%)
    pallas_call x1, Pallas kernels, shards(): pl.pallas_call(functools.partial(kernel, rows, columns), out_shape=jax.Sh...  106 us

profile of v3, /device:TPU:11, one launch (start us, length us, event | category | flops | bytes accessed | tf_op | source)
XLA Modules:
  0.0 107.7 jit_solution(13833952172120825702)
XLA Ops:
  0.0 105.6 %shard_map.55 = f32[12,128,128]{2,1,0:T(8,128)} custom-call(f32[2,2048,128]{2,1,0:T(8,128)} %bitcast.11, f32[32,128,128]{2,1,0:T(8,128)} %bitcast.12, s32[2,2,8]{2,1,0:T(2,128)} %bitcast.13, s32[4,8]{1,0:T(4,128)} %bitcast.14, s32[1,24]{1,0:T(1,128)} %bitcast.15), custom_call_target="tpu_custom_call" | custom-call | tf_op jit(solution)/shard_map/pallas_call | solution.py:477
  105.6 2.1 %copy.7 = f32[1,1,12,128,128]{4,3,2,1,0:T(8,128)} copy(f32[1,1,12,128,128]{4,3,2,1,0:T(8,128)} %bitcast.10) | data formatting | bytes 1572864

commit v4 on v3

--- a/solution.py
+++ b/solution.py
@@ -36,8 +36,8 @@
     "oA": (0, 0, IN_A), "oB": (1, IN_A, IN_B), "oD": (2, IN_A + IN_B, KB - IN_A - IN_B), "ob": (3, IN_A, IN_B),
 }
 WAITS = {
-    0: [('zE0', 2), ('zE1', 2), ('oA', 1), ('oD', 1), ('zE2', 2), ('zE3', 2), ('zA', 3), ('oB', 1), ('zD', 3), ('ob', 3)],
-    1: [('yE0', 1), ('zB', 2), ('yE1', 1), ('yE2', 1), ('zD', 2), ('yE3', 1), ('zE0', 3), ('yA', 2), ('zE2', 3), ('zE1', 3), ('zE3', 3)],
+    0: [('zE0', 2), ('zE1', 2), ('oA', 1), ('zE2', 2), ('zE3', 2), ('oD', 1), ('zA', 3), ('zD', 3), ('oB', 1), ('ob', 3)],
+    1: [('yE0', 1), ('zB', 2), ('yE1', 1), ('yE2', 1), ('zD', 2), ('yE3', 1), ('zE0', 3), ('zE1', 3), ('yA', 2), ('zE3', 3), ('zE2', 3)],
 }
 RELAYS = {
     0: {"zE0": ("yE0", 2, 1), "zE1": ("yE1", 2, 1), "zE2": ("yE2", 2, 1), "zE3": ("yE3", 2, 1),
@@ -45,20 +45,20 @@
     1: {"zB": ("ob", 2, 3), "yE0": ("zE0", 1, 3), "yE1": ("zE1", 1, 3), "yE2": ("zE2", 1, 3), "yE3": ("zE3", 1, 3)},
 }
 OWN = {
-    0: [('zE0', 2, 4), ('zE1', 2, 5), ('zE2', 2, 8), ('zE3', 2, 8)],
-    1: [('zB', 2, 5), ('oA', 1, 6), ('oD', 1, 6), ('oB', 1, 7), ('zD', 2, 10)],
+    0: [('zE0', 2, 5), ('zE1', 2, 6), ('zE2', 2, 6), ('zE3', 2, 8)],
+    1: [('zB', 2, 5), ('oA', 1, 5), ('oB', 1, 6), ('oD', 1, 6), ('zD', 2, 10)],
 }
 STEPS = 11
-PASS_ON = {0: [42, 42, 40], 1: [35, 36, 35]}
+PASS_ON = {0: [38, 39, 42], 1: [25, 38, 40]}
 LEFT_RELAY = {0: 14, 1: 14}
 LEFT_READY = {0: 17, 1: 17}
 DONE = {
-    0: [1, 2, 2, 2, 2, 2, 2, 2, 2, 2, 2, 2, 2, 2, 2, 2, 2, 4, 6, 8, 10, 10, 11, 12, 13, 14, 15, 16, 17, 18, 19, 20, 20, 23, 26, 27, 27, 27, 28, 28, 30, 30, 32, 32],
-    1: [2, 2, 2, 2, 2, 2, 2, 2, 2, 2, 2, 2, 2, 2, 2, 2, 2, 4, 6, 8, 10, 12, 13, 14, 15, 16, 17, 18, 19, 20, 21, 22, 23, 25, 26, 27, 27, 28, 29, 29, 30, 30, 31, 32],
+    0: [2, 2, 2, 2, 2, 2, 2, 2, 2, 2, 2, 2, 2, 2, 2, 2, 2, 3, 4, 5, 6, 6, 7, 8, 9, 10, 11, 12, 13, 14, 15, 16, 16, 18, 20, 22, 24, 26, 28, 28, 28, 30, 32, 32],
+    1: [1, 2, 2, 2, 2, 2, 2, 2, 2, 2, 2, 2, 2, 2, 2, 2, 2, 4, 6, 8, 10, 12, 13, 14, 15, 16, 17, 18, 19, 20, 21, 22, 23, 24, 25, 26, 27, 28, 29, 29, 30, 31, 31, 32],
 }
 ORDER = {
     0: [0, 1, 4, 5, 2, 3, 6, 7],
-    1: [0, 1, 2, 5, 3, 4, 6, 7],
+    1: [0, 1, 2, 5, 3, 6, 4, 7],
 }
 MOST = max(b - a for role in (0, 1) for a, b in zip([0] + DONE[role], DONE[role]))
 
@@ -146,7 +146,12 @@
 
     def pack(h, k):
         for slab in range(0, BS, SLAB):
-            parts = [shifted(raw[k * BPR + b, pl.ds(slab, SLAB), :], b - h) for b in range(BPR)]
+            parts = [
+                pltpu.roll(
+                    raw[k * BPR + b, pl.ds(slab, SLAB), :], lax.rem(jnp.int32(b + STRIPS) - h, STRIPS) * LANES, 1
+                )
+                for b in range(BPR)
+            ]
             units[h, 0, pl.ds(pl.multiple_of(k * BS + slab, SLAB), SLAB), :] = regroup(group, parts)
 
     def unit_copy(link, name, h, source, target):
@@ -235,13 +240,6 @@
     def _():
         x_copy(1, 0, sibling, 1).start()
 
-    def pack_rest(k, carry):
-        for h in range(1, STRIPS):
-            pack(h, k)
-        return carry
-
-    lax.fori_loop(0, KB, pack_rest, 0)
-    sums[...] = jnp.zeros_like(sums)
     small[2].wait()
 
     def row_of(tile, k):
@@ -279,8 +277,6 @@
             for turned in range(STRIPS):
                 wheres[turn_index, k, turned] = shifted(mine, STRIPS - turned)
 
-    fill_left(0)
-    fill_wheres(0)
 
     def products(h, turn_index, half):
         got = None
@@ -363,6 +359,20 @@
                             if after == at:
                                 unit_copy(link_of(own_name), own_name, h + 1, 0, target).start()
 
+        @pl.when(g == 0)
+        def _():
+            fill_left(0)
+            fill_wheres(0)
+            sums[...] = jnp.zeros_like(sums)
+
+        @pl.when((s == 1) & (h < STRIPS - 1))
+        def _():
+            def pack_next(k, c):
+                pack(h + 1, k)
+                return c
+
+            lax.fori_loop(0, KB, pack_next, 0)
+
         @pl.when(g == by_role(odd, LEFT_RELAY[0], LEFT_RELAY[1]))
         def _():
             x_copy(2, 0, left, 0).wait_recv()
@@ -374,6 +384,9 @@
             @pl.when(core == 1)
             def _():
                 x_copy(3, 2, sibling, 2).start()
+
+            fill_left(2)
+            fill_wheres(2)
 
         @pl.when(g == by_role(odd, LEFT_READY[0], LEFT_READY[1]))
         def _():
@@ -386,11 +399,11 @@
                         mark_copy(0, turn_index, inner, 0).wait_recv()
 
             def one(i, c):
-                fill_left(i)
-                fill_wheres(i)
+                fill_left(1 + 2 * i)
+                fill_wheres(1 + 2 * i)
                 return c
 
-            lax.fori_loop(1, 4, one, 0)
+            lax.fori_loop(0, 2, one, 0)
 
         for strip in range(STRIPS - 1):
             @pl.when(g == by_role(odd, PASS_ON[0][strip], PASS_ON[1][strip]))

time: 108 us -> 107 us (level)
  the two profiles are of different devices: /device:TPU:11 before, /device:TPU:1 now
where the time goes in v4:
time: 107 us; the launch traced here: 105 us
  Pallas kernels  103 us (96%)
  local copies, waits for them, and re-layouts  2.06 us (2%)
    pallas_call x1, Pallas kernels, shards(): pl.pallas_call(functools.partial(kernel, rows, columns), out_shape=jax.Sh...  103 us

profile of v4, /device:TPU:1, one launch (start us, length us, event | category | flops | bytes accessed | tf_op | source)
XLA Modules:
  0.0 104.8 jit_solution(5023784908651151071)
XLA Ops:
  0.0 102.7 %shard_map.55 = f32[12,128,128]{2,1,0:T(8,128)} custom-call(f32[2,2048,128]{2,1,0:T(8,128)} %bitcast.11, f32[32,128,128]{2,1,0:T(8,128)} %bitcast.12, s32[2,2,8]{2,1,0:T(2,128)} %bitcast.13, s32[4,8]{1,0:T(4,128)} %bitcast.14, s32[1,24]{1,0:T(1,128)} %bitcast.15), custom_call_target="tpu_custom_call" | custom-call | tf_op jit(solution)/shard_map/pallas_call | solution.py:490
  102.8 2.1 %copy.7 = f32[1,1,12,128,128]{4,3,2,1,0:T(8,128)} copy(f32[1,1,12,128,128]{4,3,2,1,0:T(8,128)} %bitcast.10) | data formatting | bytes 1572864
